TPU v7x, 256 devices: a whole 4x4x8 slice. The times are simulated.
256 devices in a mesh: reg: 64 (over z, y, core), ep: 4 (over x).
Axes of the slice: x: 4, y: 4, z: 8, core: 2. Of those that a mesh axis runs over, the one named last changes fastest.
Arguments:
- log_prices: bfloat16 [256, 64, 256], P('reg', 'ep'), may hold values from -3 to 3
- log_wages: float32 [256, 64], P('reg', 'ep'), may hold values from -12 to 1
- labor_share: float32 [256, 256], P('reg'), may hold values from 0.3 to 0.7
- io_coeffs: bfloat16 [256, 256, 256], P('reg'), may hold values from -0.375 to 0.375
- pair_blocks: bfloat16 [256, 32, 256, 256], P('reg'), may hold values from -0.0201 to 0.801
- log_tau: float32 [256, 32, 256], P('reg'), may hold values from 0.05 to 2
- elasticity: float32 [256], replicated, may hold values from 2 to 40
- partners: int32 [256, 32], replicated, may hold values from 0 to 255, as said below
- list_lengths: int32 [256], replicated, may hold values from 1 to 32, as said below
- price_cotangent: float32 [256, 64, 256], P('reg', 'ep'), may hold values from -6 to 6
Outputs:
- new_prices: bfloat16 [256, 64, 256], P('reg', 'ep')
- price_grad: float32 [256, 64, 256], P('reg', 'ep')
- wage_grad: float32 [256, 64], P('reg', 'ep')
- tau_grad: float32 [256, 32, 256], P('reg')
Inputs may be any that keep to these rules, and one draw needn't show every extreme that they name: `partners`: each list names distinct regions. Over their live entries, the 4 importers of an aligned block name at most 2 regions of any one aligned block of 4 regions, and this is reached in every draw. `list_lengths`: in some aligned block of 4 regions every list has 32 live entries.
All inputs are finite; a program needn't handle non-finite values.
Results may differ from a plain program's by a relative error of at most 0.0064.
Values may be sent and summed in bfloat16 or wider, within the bound.
A program may use at most 64 MiB of HBM per device.

v0:
```python
import jax
import jax.numpy as jnp
from jax import lax
from jax.sharding import PartitionSpec as P


def shards(
    log_prices,
    log_wages,
    labor_share,
    io_coeffs,
    pair_blocks,
    log_tau,
    elasticity,
    partners,
    list_lengths,
    price_cotangent,
):
    own_regions, episodes, sectors = log_prices.shape
    max_slots = pair_blocks.shape[1]
    slot_total = own_regions * max_slots
    row_width = episodes * sectors
    my_index = lax.axis_index("reg")
    unit_cost = (
        labor_share[:, None, :] * log_wages[:, :, None]
        + jnp.einsum("iek,ikj->iej", log_prices, io_coeffs, preferred_element_type=jnp.float32)
    ).astype(jnp.bfloat16)
    first_region = my_index * own_regions
    my_partners = lax.dynamic_slice_in_dim(partners, first_region, own_regions, 0)
    my_lengths = lax.dynamic_slice_in_dim(list_lengths, first_region, own_regions, 0)
    slot_index = jnp.arange(max_slots, dtype=jnp.int32)
    live = slot_index[None, :] < my_lengths[:, None]
    flat_partners = my_partners.reshape(-1)
    shard_rows = lax.all_gather(unit_cost, "reg", axis=0, tiled=True)
    row_count = shard_rows.shape[0]
    selector = (flat_partners[:, None] == jnp.arange(row_count, dtype=jnp.int32)[None, :]).astype(
        jnp.bfloat16
    )
    exporter_rows = jnp.dot(
        selector, shard_rows.reshape(row_count, row_width), preferred_element_type=jnp.float32
    ).astype(jnp.bfloat16)
    exporter_rows = exporter_rows.reshape(own_regions, max_slots, episodes, sectors)
    landed = log_tau[:, :, None, :] + jnp.einsum(
        "rsek,rskj->rsej", exporter_rows, pair_blocks, preferred_element_type=jnp.float32
    )
    live_mask = live[:, :, None, None]
    scores = jnp.where(live_mask, -elasticity * landed, -jnp.inf)
    top_score = jnp.max(scores, axis=1)
    weights = jnp.exp(scores - top_score[:, None])
    total = jnp.sum(weights, axis=1)
    new_prices = (-(top_score + jnp.log(total)) / elasticity).astype(jnp.bfloat16)
    adjoint = price_cotangent[:, None] * (weights / total[:, None])
    tau_grad = lax.psum(jnp.sum(adjoint, axis=2), "ep")
    pushed = jnp.einsum(
        "rsej,rskj->rsek",
        adjoint.astype(jnp.bfloat16),
        pair_blocks,
        preferred_element_type=jnp.float32,
    ).astype(jnp.bfloat16)
    pushed = jnp.where(live_mask, pushed, jnp.zeros((), jnp.bfloat16)).reshape(
        slot_total, row_width
    )
    selector = (
        jnp.arange(own_regions * lax.axis_size("reg"), dtype=jnp.int32)[:, None]
        == flat_partners[None, :]
    ).astype(jnp.bfloat16)
    cost_adjoint = lax.psum_scatter(
        jnp.dot(selector, pushed, preferred_element_type=jnp.float32),
        "reg",
        scatter_dimension=0,
        tiled=True,
    )
    cost_adjoint = cost_adjoint.reshape(own_regions, episodes, sectors)
    price_grad = jnp.einsum(
        "iej,ikj->iek",
        cost_adjoint.astype(jnp.bfloat16),
        io_coeffs,
        preferred_element_type=jnp.float32,
    )
    wage_grad = jnp.sum(cost_adjoint * labor_share[:, None, :], axis=2)
    return (new_prices, price_grad, wage_grad, tau_grad)


def solution(mesh):
    return jax.shard_map(
        shards,
        mesh=mesh,
        in_specs=(
            P("reg", "ep", None),
            P("reg", "ep"),
            P("reg", None),
            P("reg", None, None),
            P("reg", None, None, None),
            P("reg", None, None),
            P(),
            P(),
            P(),
            P("reg", "ep", None),
        ),
        out_specs=(
            P("reg", "ep", None),
            P("reg", "ep", None),
            P("reg", "ep"),
            P("reg", None, None),
        ),
        check_vma=False,
    )
```

profile of v0, /device:TPU:8, one launch (start us, length us, event | category | flops | bytes accessed | tf_op | source)
XLA Modules:
  0.0 369.9 jit_solution(17830627746724783566)
XLA Ops:
  7.2 0.0 copy-start
  7.2 0.0 all-gather.2.cloned.1.call-start
  7.2 1.0 copy-done
  8.2 1.6 fusion.2
  9.8 0.0 all-gather.2.cloned.1.call-update
  9.8 0.0 all-reduce.6.cloned.1.call-start
  9.9 0.7 neg.6
  10.6 0.8 dynamic_slice.6
  11.3 0.8 constant_dynamic-slice_fusion.1
  12.1 0.1 copy.15
  12.2 0.1 eq.28
  12.3 0.1 iota_compare_fusion.4
  12.3 78.3 %all-gather.2.cloned.1.call-done = bf16[256,16,256]{2,1,0:T(8,128)(2,1)} async-done(((bf16[4,16,256]{2,1,0:T(8,128)(2,1)}), bf16[256,16,256]{2,1,0:T(8,128)(2,1)}) %all-gather.2.cloned.1.call-update) | async-done | bytes 2097168 | tf_op jit(solution)/shard_map/all_gather | solution.py:34
  90.6 2.5 copy.16
  93.2 0.0 copy-start.2
  93.2 0.5 convolution_convert_fusion
  93.7 0.2 copy.17
  93.9 0.1 copy-done.2
  94.1 8.1 %fusion.11 = (f32[4,16,256]{2,1,0:T(8,128)S(1)}, f32[4,32,16,256]{3,2,1,0:T(8,128)S(1)}) fusion(bf16[4,32,256,256]{3,2,1,0:T(8,128)(2,1)} %param.14, f32[4,32,256]{2,1,0:T(8,128)S(1)} %copy-done.2, f32[256]{0:T(256)S(1)} %neg.6, pred[4,32]{1,0:T(4,128)(4,1)S(1)} %iota_compare_fusion.4, bf16[4,32,16,256]{3,2,1,0:T(8,128)(2,1)S(1)} %bitcast.31), kind=kOutput, calls=%fused_computation.25 | convolution fusion | flops 270516224 | bytes 20120704 | tf_op jit(solution)/shard_map/rsek,rskj->rsej/dot_general | solution.py:43
  102.2 0.0 copy-start.1
  102.2 0.3 fusion
  102.5 0.5 copy-done.1
  103.1 11.2 %fusion.1 = bf16[4,32,16,256]{3,2,1,0:T(8,128)(2,1)} fusion(bf16[4,32,256,256]{3,2,1,0:T(8,128)(2,1)} %param.14, pred[4,32]{1,0:T(4,128)(4,1)S(1)} %iota_compare_fusion.4, f32[4,32,16,256]{3,2,1,0:T(8,128)S(1)} %get-tuple-element.5, f32[4,16,256]{2,1,0:T(8,128)S(1)} %fusion, f32[4,16,256]{2,1,0:T(8,128)S(1)} %copy-done.1, f32[4,16,256]{2,1,0:T(8,128)S(1)} %get-tuple-element.4), kind=kOutput, calls=%fused_computation.6 | convolution fusion | flops 271581184 | bytes 20119680 | tf_op jit(solution)/shard_map/rsej,rskj->rsek/dot_general | solution.py:54
  114.3 1.6 copy.18
  116.0 2.7 fusion.6
  118.6 0.0 copy-start.5
  118.6 0.0 copy-start.4
  118.6 0.0 all-reduce.6.cloned.1.call-update
  118.7 0.0 copy-start.3
  118.7 0.0 all-reduce.4.cloned.1.call-start
  118.7 0.6 copy-done.5
  119.3 0.6 dynamic-slice
  120.5 0.0 copy-done.4
  120.5 0.6 divide_convert_fusion
  121.2 1.3 fusion.5
  122.5 0.0 all-reduce.4.cloned.1.call-update
  122.5 191.0 %all-reduce.6.cloned.1.call-done = f32[256,4096]{1,0:T(8,128)} async-done(((f32[256,4096]{1,0:T(8,128)}), f32[256,4096]{1,0:T(8,128)}) %all-reduce.6.cloned.1.call-update) | async-done | bytes 4194320
  313.5 0.9 constant_dynamic-slice_fusion
  314.5 0.9 fusion.10
  315.3 0.0 copy-done.3
  315.4 0.7 fusion.7
  316.0 45.7 %all-reduce.4.cloned.1.call-done = f32[4,32,256]{2,1,0:T(8,128)} async-done(((f32[4,32,256]{2,1,0:T(8,128)}), f32[4,32,256]{2,1,0:T(8,128)}) %all-reduce.4.cloned.1.call-update) | async-done | bytes 131088 | tf_op jit(solution)/shard_map/psum | solution.py:53
  361.8 1.6 copy.25
Async XLA Ops:
  7.2 1.0 copy-start
  7.2 83.5 %all-gather.2.cloned.1.call-start = ((), (), s32[]{:S(2)}) async-start(), calls=%async_computation | async-start | bytes 2129920 | tf_op jit(solution)/shard_map/all_gather | solution.py:34
  9.8 303.7 %all-reduce.6.cloned.1.call-start = ((), (), s32[]{:S(2)}) async-start(), calls=%async_computation.2 | async-start | bytes 8388608
  93.2 0.9 copy-start.2
  102.2 0.8 copy-start.1
  118.6 0.7 copy-start.5
  118.6 1.9 copy-start.4
  118.7 196.7 %copy-start.3 = (f32[4,256]{1,0:T(4,128)S(1)}, f32[4,256]{1,0:T(4,128)}, u32[]{:S(2)}) copy-start(f32[4,256]{1,0:T(4,128)} %param.12) | copy-start | bytes 12292
  118.7 243.1 %all-reduce.4.cloned.1.call-start = ((), (), s32[]{:S(2)}) async-start(), calls=%async_computation.1 | async-start | bytes 262144 | tf_op jit(solution)/shard_map/psum | solution.py:53
Sparse Core Ops, SparseCore 0:
  11.3 79.2 all-gather.1
  118.8 194.7 all-reduce.5
  316.4 45.2 all-reduce.3
where the time goes:
time: 370 us
  waiting for transfers between devices  315 us (85%)
  matrix products  25 us (7%)
  between operations  14.5 us (4%)
  local copies, waits for them, and re-layouts  11.5 us (3%)
    unnamed x4, waiting for transfers between devices  191 us
    all_gather x1, waiting for transfers between devices, shards(): shard_rows = lax.all_gather(unit_cost, 'reg', axis=0, tiled=True)  78.3 us
    psum x1, waiting for transfers between devices, shards(): tau_grad = lax.psum(jnp.sum(adjoint, axis=2), 'ep')  45.7 us
    dot_general x1, matrix products, shards(): jnp.einsum('rsej,rskj->rsek', adjoint.astype(jnp.bfloat16), pair_blocks,...  11.2 us
    unnamed x18, local copies, waits for them, and re-layouts  9.77 us
    dot_general x1, matrix products, shards(): jnp.einsum('rsek,rskj->rsej', exporter_rows, pair_blocks, preferred_eleme...  8.14 us
  transfers between devices with their start and end apart: 3, of which 3 were waited for; matrix products, arithmetic and copies ran while one was open for 2% of the time, Pallas kernels for 0%

commit v1 on v0

--- a/solution.py
+++ b/solution.py
@@ -50,7 +50,7 @@
     total = jnp.sum(weights, axis=1)
     new_prices = (-(top_score + jnp.log(total)) / elasticity).astype(jnp.bfloat16)
     adjoint = price_cotangent[:, None] * (weights / total[:, None])
-    tau_grad = lax.psum(jnp.sum(adjoint, axis=2), "ep")
+    tau_grad = jnp.sum(lax.all_gather(jnp.sum(adjoint, axis=2), "ep"), axis=0)
     pushed = jnp.einsum(
         "rsej,rskj->rsek",
         adjoint.astype(jnp.bfloat16),

time: 370 us -> 324 us (0.88)
  waiting for transfers between devices: 315 us -> 256 us
  blocking collectives: 0 us -> 13.1 us
    psum x1 -> x0, waiting for transfers between devices: 45.7 us -> none  [shards(): tau_grad = lax.psum(jnp.sum(adjoint, axis=2), 'ep')]
    unnamed x4 -> x3, waiting for transfers between devices: 191 us -> 178 us
    all_gather x0 -> x1, blocking collectives: none -> 13.1 us  [shards(): tau_grad = jnp.sum(lax.all_gather(jnp.sum(adjoint, axis=2), 'ep'), axis=0)]
    unnamed x18 -> x17, local copies, waits for them, and re-layouts: 9.77 us -> 8.24 us
  transfers between devices with their start and end apart: 3 -> 2, of which waited for: 3 -> 2; matrix products, arithmetic and copies ran while one was open for 2% -> 2% of each run, Pallas kernels for 0% -> 0%
where the time goes in v1:
time: 324 us; the launch traced here: 323 us
  waiting for transfers between devices  256 us (79%)
  matrix products  25 us (8%)
  between operations  14.8 us (5%)
  blocking collectives  13.1 us (4%)
  local copies, waits for them, and re-layouts  9.94 us (3%)
  other arithmetic  3.73 us (1%)
    unnamed x3, waiting for transfers between devices  178 us
    all_gather x1, waiting for transfers between devices, shards(): shard_rows = lax.all_gather(unit_cost, 'reg', axis=0, tiled=True)  78.3 us
    all_gather x1, blocking collectives, shards(): tau_grad = jnp.sum(lax.all_gather(jnp.sum(adjoint, axis=2), 'ep'), axis=0)  13.1 us
    dot_general x1, matrix products, shards(): jnp.einsum('rsej,rskj->rsek', adjoint.astype(jnp.bfloat16), pair_blocks,...  11.2 us
    unnamed x17, local copies, waits for them, and re-layouts  8.24 us
    dot_general x1, matrix products, shards(): jnp.einsum('rsek,rskj->rsej', exporter_rows, pair_blocks, preferred_eleme...  8.14 us
  transfers between devices with their start and end apart: 2, of which 2 were waited for; matrix products, arithmetic and copies ran while one was open for 2% of the time, Pallas kernels for 0%

profile of v1, /device:TPU:8, one launch (start us, length us, event | category | flops | bytes accessed | tf_op | source)
XLA Modules:
  0.0 322.9 jit_solution(4442986376792780842)
XLA Ops:
  7.2 0.0 copy-start
  7.2 0.0 all-gather.3.cloned.1.call-start
  7.2 1.0 copy-done
  8.2 1.6 fusion.2
  9.8 0.0 all-gather.3.cloned.1.call-update
  9.8 0.0 all-reduce.3.cloned.1.call-start
  9.9 0.7 neg.6
  10.6 0.8 dynamic_slice.6
  11.3 0.8 constant_dynamic-slice_fusion.1
  12.1 0.1 copy.15
  12.2 0.1 eq.28
  12.3 0.1 iota_compare_fusion.4
  12.3 78.3 %all-gather.3.cloned.1.call-done = bf16[256,16,256]{2,1,0:T(8,128)(2,1)} async-done(((bf16[4,16,256]{2,1,0:T(8,128)(2,1)}), bf16[256,16,256]{2,1,0:T(8,128)(2,1)}) %all-gather.3.cloned.1.call-update) | async-done | bytes 2097168 | tf_op jit(solution)/shard_map/all_gather | solution.py:34
  90.6 2.5 copy.16
  93.2 0.0 copy-start.2
  93.2 0.5 convolution_convert_fusion
  93.7 0.2 copy.17
  93.9 0.1 copy-done.2
  94.1 8.1 %fusion.11 = (f32[4,16,256]{2,1,0:T(8,128)S(1)}, f32[4,32,16,256]{3,2,1,0:T(8,128)S(1)}) fusion(bf16[4,32,256,256]{3,2,1,0:T(8,128)(2,1)} %param.14, f32[4,32,256]{2,1,0:T(8,128)S(1)} %copy-done.2, f32[256]{0:T(256)S(1)} %neg.6, pred[4,32]{1,0:T(4,128)(4,1)S(1)} %iota_compare_fusion.4, bf16[4,32,16,256]{3,2,1,0:T(8,128)(2,1)S(1)} %bitcast.32), kind=kOutput, calls=%fused_computation.25 | convolution fusion | flops 270516224 | bytes 20120704 | tf_op jit(solution)/shard_map/rsek,rskj->rsej/dot_general | solution.py:43
  102.2 0.0 copy-start.1
  102.2 0.3 fusion
  102.5 0.5 copy-done.1
  103.1 11.2 %fusion.1 = bf16[4,32,16,256]{3,2,1,0:T(8,128)(2,1)} fusion(bf16[4,32,256,256]{3,2,1,0:T(8,128)(2,1)} %param.14, pred[4,32]{1,0:T(4,128)(4,1)S(1)} %iota_compare_fusion.4, f32[4,32,16,256]{3,2,1,0:T(8,128)S(1)} %get-tuple-element.5, f32[4,16,256]{2,1,0:T(8,128)S(1)} %fusion, f32[4,16,256]{2,1,0:T(8,128)S(1)} %copy-done.1, f32[4,16,256]{2,1,0:T(8,128)S(1)} %get-tuple-element.4), kind=kOutput, calls=%fused_computation.6 | convolution fusion | flops 271581184 | bytes 20119680 | tf_op jit(solution)/shard_map/rsej,rskj->rsek/dot_general | solution.py:54
  114.3 1.6 copy.18
  116.0 2.7 fusion.6
  118.6 0.0 copy-start.5
  118.6 0.0 all-reduce.3.cloned.1.call-update
  118.7 0.0 copy-start.4
  118.7 0.0 copy-start.3
  118.7 0.6 copy-done.5
  119.3 0.6 dynamic-slice
  120.5 0.7 fusion.5
  121.2 13.1 %all-gather = f32[16,32,256]{2,1,0:T(8,128)S(1)} all-gather(f32[4,32,256]{2,1,0:T(8,128)S(1)} %fusion.5), channel_id=2, replica_groups=mesh['reg'=64,'ep'=4] {'ep'}, dimensions={0}, use_global_device_ids=true | all-gather | bytes 655360 | tf_op jit(solution)/shard_map/all_gather | solution.py:53
  134.3 0.7 reduce_sum.39
  135.0 0.0 copy-done.4
  135.0 0.6 divide_convert_fusion
  135.7 177.9 %all-reduce.3.cloned.1.call-done = f32[256,4096]{1,0:T(8,128)} async-done(((f32[256,4096]{1,0:T(8,128)}), f32[256,4096]{1,0:T(8,128)}) %all-reduce.3.cloned.1.call-update) | async-done | bytes 4194320
  313.5 0.9 constant_dynamic-slice_fusion
  314.5 0.0 copy-done.3
  314.5 0.7 fusion.7
  315.1 0.9 fusion.10
Async XLA Ops:
  7.2 1.0 copy-start
  7.2 83.5 %all-gather.3.cloned.1.call-start = ((), (), s32[]{:S(2)}) async-start(), calls=%async_computation | async-start | bytes 2129920 | tf_op jit(solution)/shard_map/all_gather | solution.py:34
  9.8 303.7 %all-reduce.3.cloned.1.call-start = ((), (), s32[]{:S(2)}) async-start(), calls=%async_computation.1 | async-start | bytes 8388608
  93.2 0.9 copy-start.2
  102.2 0.8 copy-start.1
  118.6 0.7 copy-start.5
  118.7 16.4 %copy-start.4 = (f32[256]{0:T(256)S(1)}, f32[256]{0:T(256)}, u32[]{:S(2)}) copy-start(f32[256]{0:T(256)} %param.16) | copy-start | bytes 3076
  118.7 195.8 %copy-start.3 = (f32[4,256]{1,0:T(4,128)S(1)}, f32[4,256]{1,0:T(4,128)}, u32[]{:S(2)}) copy-start(f32[4,256]{1,0:T(4,128)} %param.12) | copy-start | bytes 12292
Sparse Core Ops, SparseCore 0:
  11.3 79.2 all-gather.2
  118.8 194.7 all-reduce.2

commit v2 on v0

--- a/solution.py
+++ b/solution.py
@@ -31,7 +31,9 @@
     slot_index = jnp.arange(max_slots, dtype=jnp.int32)
     live = slot_index[None, :] < my_lengths[:, None]
     flat_partners = my_partners.reshape(-1)
-    shard_rows = lax.all_gather(unit_cost, "reg", axis=0, tiled=True)
+    shard_rows = jnp.concatenate(
+        lax.all_to_all(jnp.stack([unit_cost] * lax.axis_size("reg")), "reg", 0, 0), axis=0
+    )
     row_count = shard_rows.shape[0]
     selector = (flat_partners[:, None] == jnp.arange(row_count, dtype=jnp.int32)[None, :]).astype(
         jnp.bfloat16

time: 370 us -> 351 us (0.949)
  waiting for transfers between devices: 315 us -> 285 us
  starting transfers between devices: 0.12 us -> 12.3 us
    all_gather x1 -> x0, waiting for transfers between devices: 78.3 us -> none  [shards(): shard_rows = lax.all_gather(unit_cost, 'reg', axis=0, tiled=True)]
    all_to_all x0 -> x1, waiting for transfers between devices: none -> 50.8 us  [shards(): lax.all_to_all(jnp.stack([unit_cost] * lax.axis_size('reg')), 'reg', 0, 0)]
    all_to_all x0 -> x1, starting transfers between devices: none -> 12.2 us  [shards(): lax.all_to_all(jnp.stack([unit_cost] * lax.axis_size('reg')), 'reg', 0, 0)]
    unnamed x4 -> x3, waiting for transfers between devices: 191 us -> 189 us
    unnamed x18 -> x22, local copies, waits for them, and re-layouts: 9.77 us -> 8.23 us
where the time goes in v2:
time: 351 us; the launch traced here: 350 us
  waiting for transfers between devices  285 us (81%)
  matrix products  24.4 us (7%)
  between operations  14.8 us (4%)
  starting transfers between devices  12.3 us (4%)
  local copies, waits for them, and re-layouts  10.2 us (3%)
    unnamed x3, waiting for transfers between devices  189 us
    all_to_all x1, waiting for transfers between devices, shards(): lax.all_to_all(jnp.stack([unit_cost] * lax.axis_size('reg')), 'reg', 0, 0)  50.8 us
    psum x1, waiting for transfers between devices, shards(): tau_grad = lax.psum(jnp.sum(adjoint, axis=2), 'ep')  45.7 us
    all_to_all x1, starting transfers between devices, shards(): lax.all_to_all(jnp.stack([unit_cost] * lax.axis_size('reg')), 'reg', 0, 0)  12.2 us
    dot_general x1, matrix products, shards(): jnp.einsum('rsej,rskj->rsek', adjoint.astype(jnp.bfloat16), pair_blocks,...  11.2 us
    unnamed x22, local copies, waits for them, and re-layouts  8.23 us
    dot_general x1, matrix products, shards(): jnp.einsum('rsek,rskj->rsej', exporter_rows, pair_blocks, preferred_eleme...  8.14 us
  transfers between devices with their start and end apart: 3, of which 3 were waited for; matrix products, arithmetic and copies ran while one was open for 2% of the time, Pallas kernels for 0%

profile of v2, /device:TPU:8, one launch (start us, length us, event | category | flops | bytes accessed | tf_op | source)
XLA Modules:
  0.0 350.0 jit_solution(6359894717896498066)
XLA Ops:
  7.2 0.0 copy-start
  7.2 1.0 copy-done
  8.2 1.0 fusion.2
  9.2 1.6 stack.2
  10.8 0.0 copy-start.5
  10.8 0.0 copy-start.6
  10.8 0.0 copy-start.4
  10.8 12.2 %all-to-all-start = ((bf16[64,4,16,256]{3,2,1,0:T(8,128)(2,1)}), bf16[64,4,16,256]{3,2,1,0:T(8,128)(2,1)S(1)}, u32[]{:S(2)}, u32[]{:S(2)}) async-start(bf16[64,4,16,256]{3,2,1,0:T(8,128)(2,1)} %stack.2), calls=%async_computation | async-start | bytes 4194304 | tf_op jit(solution)/shard_map/all_to_all | solution.py:35
  23.0 0.0 all-reduce.6.cloned.1.call-start
  23.1 0.0 copy-done.5
  23.1 0.0 copy-done.6
  23.1 0.1 dynamic_slice.6
  23.2 0.0 copy-done.4
  23.2 0.1 constant_dynamic-slice_fusion.1
  23.3 0.1 copy.15
  23.3 0.1 eq.28
  23.4 0.1 iota_compare_fusion.4
  23.5 50.8 %all-to-all-done = bf16[64,4,16,256]{3,2,1,0:T(8,128)(2,1)S(1)} async-done(((bf16[64,4,16,256]{3,2,1,0:T(8,128)(2,1)}), bf16[64,4,16,256]{3,2,1,0:T(8,128)(2,1)S(1)}, u32[]{:S(2)}, u32[]{:S(2)}) %all-to-all-start) | async-done | bytes 2097184 | tf_op jit(solution)/shard_map/all_to_all | solution.py:35
  74.3 0.9 copy.16
  75.2 0.0 copy-start.2
  75.2 0.5 convolution_convert_fusion
  75.7 0.2 copy.17
  76.0 0.1 copy-done.2
  76.1 8.1 %fusion.11 = (f32[4,16,256]{2,1,0:T(8,128)S(1)}, f32[4,32,16,256]{3,2,1,0:T(8,128)S(1)}) fusion(bf16[4,32,256,256]{3,2,1,0:T(8,128)(2,1)} %param.14, f32[4,32,256]{2,1,0:T(8,128)S(1)} %copy-done.2, f32[256]{0:T(256)S(1)} %neg.6, pred[4,32]{1,0:T(4,128)(4,1)S(1)} %iota_compare_fusion.4, bf16[4,32,16,256]{3,2,1,0:T(8,128)(2,1)S(1)} %bitcast.33), kind=kOutput, calls=%fused_computation.25 | convolution fusion | flops 270516224 | bytes 20120704 | tf_op jit(solution)/shard_map/rsek,rskj->rsej/dot_general | solution.py:45
  84.3 0.0 copy-start.1
  84.3 0.3 fusion
  84.6 0.5 copy-done.1
  85.1 11.2 %fusion.1 = bf16[4,32,16,256]{3,2,1,0:T(8,128)(2,1)} fusion(bf16[4,32,256,256]{3,2,1,0:T(8,128)(2,1)} %param.14, pred[4,32]{1,0:T(4,128)(4,1)S(1)} %iota_compare_fusion.4, f32[4,32,16,256]{3,2,1,0:T(8,128)S(1)} %get-tuple-element.5, f32[4,16,256]{2,1,0:T(8,128)S(1)} %fusion, f32[4,16,256]{2,1,0:T(8,128)S(1)} %copy-done.1, f32[4,16,256]{2,1,0:T(8,128)S(1)} %get-tuple-element.4), kind=kOutput, calls=%fused_computation.6 | convolution fusion | flops 271581184 | bytes 20119680 | tf_op jit(solution)/shard_map/rsej,rskj->rsek/dot_general | solution.py:56
  96.3 1.6 copy.18
  98.0 2.7 fusion.6
  100.7 0.0 copy-start.7
  100.7 0.0 all-reduce.6.cloned.1.call-update
  100.7 0.0 copy-start.3
  100.7 0.0 all-reduce.4.cloned.1.call-start
  100.7 0.6 copy-done.7
  101.3 0.6 dynamic-slice
  102.6 0.6 divide_convert_fusion
  103.2 1.3 fusion.5
  104.5 0.0 all-reduce.4.cloned.1.call-update
  104.6 188.9 %all-reduce.6.cloned.1.call-done = f32[256,4096]{1,0:T(8,128)} async-done(((f32[256,4096]{1,0:T(8,128)}), f32[256,4096]{1,0:T(8,128)}) %all-reduce.6.cloned.1.call-update) | async-done | bytes 4194320
  293.4 0.9 constant_dynamic-slice_fusion
  294.3 0.9 fusion.10
  295.2 0.0 copy-done.3
  295.2 0.7 fusion.7
  295.9 45.7 %all-reduce.4.cloned.1.call-done = f32[4,32,256]{2,1,0:T(8,128)} async-done(((f32[4,32,256]{2,1,0:T(8,128)}), f32[4,32,256]{2,1,0:T(8,128)}) %all-reduce.4.cloned.1.call-update) | async-done | bytes 131088 | tf_op jit(solution)/shard_map/psum | solution.py:55
  341.6 1.6 copy.25
  (1 shorter events, 0.0 us)
Async XLA Ops:
  7.2 1.0 copy-start
  10.8 12.3 %copy-start.5 = (f32[256]{0:T(256)S(1)}, f32[256]{0:T(256)}, u32[]{:S(2)}) copy-start(f32[256]{0:T(256)} %param.16) | copy-start | bytes 3076
  10.8 12.3 %copy-start.6 = (s32[256]{0:T(256)S(1)}, s32[256]{0:T(256)}, u32[]{:S(2)}) copy-start(s32[256]{0:T(256)} %param.18) | copy-start | bytes 3076
  10.8 12.4 %copy-start.4 = (s32[256,32]{0,1:T(8,128)S(1)}, s32[256,32]{0,1:T(8,128)}, u32[]{:S(2)}) copy-start(s32[256,32]{0,1:T(8,128)} %param.17) | copy-start | bytes 98308
  10.8 63.5 %all-to-all-start = ((bf16[64,4,16,256]{3,2,1,0:T(8,128)(2,1)}), bf16[64,4,16,256]{3,2,1,0:T(8,128)(2,1)S(1)}, u32[]{:S(2)}, u32[]{:S(2)}) async-start(bf16[64,4,16,256]{3,2,1,0:T(8,128)(2,1)} %stack.2), calls=%async_computation | async-start | bytes 4194304 | tf_op jit(solution)/shard_map/all_to_all | solution.py:35
  23.0 270.4 %all-reduce.6.cloned.1.call-start = ((), (), s32[]{:S(2)}) async-start(), calls=%async_computation.2 | async-start | bytes 8388608
  75.2 0.9 copy-start.2
  84.3 0.8 copy-start.1
  100.7 0.7 copy-start.7
  100.7 194.5 %copy-start.3 = (f32[4,256]{1,0:T(4,128)S(1)}, f32[4,256]{1,0:T(4,128)}, u32[]{:S(2)}) copy-start(f32[4,256]{1,0:T(4,128)} %param.12) | copy-start | bytes 12292
  100.7 240.9 %all-reduce.4.cloned.1.call-start = ((), (), s32[]{:S(2)}) async-start(), calls=%async_computation.1 | async-start | bytes 262144 | tf_op jit(solution)/shard_map/psum | solution.py:55
Sparse Core Ops, SparseCore 0:
  100.8 192.5 all-reduce.5
  296.3 45.2 all-reduce.3
